TPU v7x, 256 devices: a whole 4x4x8 slice. The times are simulated.
256 devices in a mesh: blk: 32 (over x, z), leaf: 4 (over y), samp: 2 (over core).
Axes of the slice: x: 4, y: 4, z: 8, core: 2. Of those that a mesh axis runs over, the one named last changes fastest.
Arguments:
- points: float32 [3, 32768], P(None, ('blk', 'leaf')), may hold values from 0 to 64, as said below
- neighbors: int32 [128, 8], P(('blk', 'leaf')), may hold values from -1 to 127, as said below
- omega: float32 [512, 32768], P(None, ('blk', 'leaf')), may hold values from -6 to 6
- observed: float32 [32768], P(('blk', 'leaf')), may hold values from -6 to 6
- prior_draws: float32 [64, 32768], P('samp', ('blk', 'leaf')), may hold values from -6 to 6
Outputs:
- weights: float32 [64, 32768], P('samp', ('blk', 'leaf'))
- residual: float32 [64, 32768], P('samp', ('blk', 'leaf'))
Inputs may be any that keep to these rules, and one draw needn't show every extreme that they name: Block g's points lie in the unit cell with integer corner (cx, cy, cz), where cx // 2 = g // 4 and 0 <= cy, cz < 3. `neighbors`: row g lists in ascending order every block h whose unit cell touches g's (cells at most one apart in every coordinate, the first taken periodic of period 2 * 32), which includes every block with a point within distance 1 of a point of g, followed by -1 in the unused slots; the relation is symmetric, and every listed block has a slab index h // 4 equal to or cyclically next to g // 4.
All inputs are finite; a program needn't handle non-finite values.
Results may differ from a plain program's by a relative error of at most 0.0003.
Values sent between devices are 32-bit elements; how exact they have to be, the bound alone decides.
A program may use at most 64 MiB of HBM per device.

v0:
```python
import jax
import jax.numpy as jnp
from jax import lax
from jax.sharding import PartitionSpec as P

PB = 256
ITERS = 2
support_radius = 0.8
noise_variance = 1.0
sketch_shift = 1.0
ALL_AXES = ("blk", "leaf", "samp")


def shifted_2(block, axis, distance):
    devices = range(lax.axis_size(axis))
    route = [((i - distance) % len(devices), i) for i in devices]
    return lax.ppermute(block, axis, route)


def wendland(row_points, column_points, period):
    offset = row_points[None, :, :, None] - column_points[:, :, None, :]
    half_period = 0.5 * period
    along_x = jnp.mod(offset[:, 0] + half_period, period) - half_period
    squared = along_x * along_x + offset[:, 1] * offset[:, 1] + offset[:, 2] * offset[:, 2]
    radius = jnp.sqrt(squared) / support_radius
    remain = jnp.maximum(1.0 - radius, 0.0)
    return remain**4 * (4.0 * radius + 1.0)


def high_dot(left, right):
    return jnp.dot(left, right, precision=lax.Precision.HIGHEST, preferred_element_type=jnp.float32)


def shifted(values, offset_by):
    return shifted_2(values, "blk", offset_by)


def beside_all(values):
    slab_values = lax.all_gather(values, "leaf", axis=1, tiled=True)
    return jnp.concatenate([shifted(slab_values, 1), slab_values, shifted(slab_values, -1)], axis=1)


def lower_solve(factor, values):
    return lax.linalg.triangular_solve(factor, values, left_side=True, lower=True)


def local(points, neighbors, omega, observed, prior_draws):
    blk_dev = neighbors.shape[0]
    cycle_count = lax.axis_size("blk")
    slab_blocks = blk_dev * lax.axis_size("leaf")
    period = 2.0 * cycle_count
    own_slab = lax.axis_index("blk")
    n_samp = lax.axis_size("samp")
    samp_idx = lax.axis_index("samp")
    usable = neighbors >= 0
    relative = jnp.mod(neighbors // slab_blocks - own_slab + 1, cycle_count)
    chosen = jnp.where(usable, relative * slab_blocks + jnp.mod(neighbors, slab_blocks), 0)
    usable_weight = usable.astype(jnp.float32)
    reach_points = beside_all(points)
    reach_blocks = reach_points.reshape(3, 3 * slab_blocks, PB).transpose(1, 0, 2)
    row_blocks = points.reshape(3, blk_dev, PB).transpose(1, 0, 2)
    kernel_tile = wendland(row_blocks[0], reach_blocks[chosen[0]], period)
    kernel_tile = kernel_tile * usable_weight[0][:, None, None]

    def apply_kernel(values):
        width = values.shape[0]
        reach = beside_all(values).reshape(width, 3 * slab_blocks, PB)
        picked = jnp.take(reach, chosen[0], axis=1)
        return jnp.einsum("cnj,nij->ci", picked, kernel_tile, precision=lax.Precision.HIGHEST)

    def slot(x):
        zeros = jnp.zeros((n_samp,) + x.shape, x.dtype)
        return lax.dynamic_update_index_in_dim(zeros, x, samp_idx, 0)

    def unslot(xs):
        return lax.dynamic_index_in_dim(xs, samp_idx, 0, keepdims=False)

    def total_per_samp(values):
        return jax.tree.map(unslot, lax.psum(jax.tree.map(slot, values), ALL_AXES))

    sketch = apply_kernel(omega) + sketch_shift * omega
    rhs = observed[None, :] - prior_draws
    half = PB // n_samp
    omega_half = lax.dynamic_slice_in_dim(omega, samp_idx * half, half, axis=1)
    sketch_half = lax.dynamic_slice_in_dim(sketch, samp_idx * half, half, axis=1)
    core_part = high_dot(omega_half, sketch_half.T)
    square_part = high_dot(sketch_half, sketch_half.T)
    joint_part = 0.5 * (core_part + core_part.T) + 0.5 * (square_part + square_part.T)
    rhs_part = slot(high_dot(sketch, rhs.T))
    joint_gram, rhs_proj = lax.psum((joint_part, rhs_part), ALL_AXES)
    rhs_proj = unslot(rhs_proj)
    joint_factor = jnp.linalg.cholesky(joint_gram)

    def precond_from(vectors, projected):
        first_solve = lower_solve(joint_factor, projected)
        solved = lax.linalg.triangular_solve(
            joint_factor, first_solve, left_side=True, lower=True, transpose_a=True
        )
        return (vectors - high_dot(solved.T, sketch)) / noise_variance

    residual = rhs
    projected = rhs_proj
    precond = precond_from(residual, projected)
    direction = precond
    weights = jnp.zeros_like(rhs)
    image = apply_kernel(direction) + noise_variance * direction
    inner_now, curvature, image_proj = total_per_samp(
        (
            jnp.sum(residual * precond, axis=1),
            jnp.sum(direction * image, axis=1),
            high_dot(sketch, image.T),
        )
    )
    step_size = inner_now / curvature
    weights = weights + step_size[:, None] * direction
    residual = residual - step_size[:, None] * image
    projected = projected - step_size[None, :] * image_proj
    precond = precond_from(residual, projected)
    inner_next = total_per_samp(jnp.sum(residual * precond, axis=1))
    direction = precond + (inner_next / inner_now)[:, None] * direction
    inner_now = inner_next
    image = apply_kernel(direction) + noise_variance * direction
    curvature = total_per_samp(jnp.sum(direction * image, axis=1))
    step_size = inner_now / curvature
    weights = weights + step_size[:, None] * direction
    residual = residual - step_size[:, None] * image
    return (weights, residual)


def solution(mesh):
    in_specs = (
        P(None, ("blk", "leaf")),
        P(("blk", "leaf"), None),
        P(None, ("blk", "leaf")),
        P(("blk", "leaf")),
        P("samp", ("blk", "leaf")),
    )
    out_specs = (P("samp", ("blk", "leaf")), P("samp", ("blk", "leaf")))
    return jax.shard_map(local, mesh=mesh, in_specs=in_specs, out_specs=out_specs, check_vma=False)
```

profile of v0, /device:TPU:1, one launch (start us, length us, event | category | flops | bytes accessed | tf_op | source)
XLA Modules:
  0.0 1005.4 jit_solution(9335899095662480256)
XLA Ops:
  9.3 10.5 %all_gather.13 = f32[3,1024]{1,0:T(4,128)S(1)} all-gather(f32[3,256]{1,0:T(4,128)} %param.11), channel_id=1, replica_groups=mesh['blk'=32,'leaf'=4,'samp'=2] {'leaf'}, dimensions={1}, use_global_device_ids=true | all-gather | bytes 15360 | tf_op jit(solution)/shard_map/all_gather | solution.py:39
  19.9 7.8 collective-permute-start.3
  27.6 19.4 %all-gather.2.cloned.1.call-done = f32[512,1024]{0,1:T(8,128)} async-done(((f32[512,256]{0,1:T(8,128)}), f32[512,1024]{0,1:T(8,128)}) %all-gather.2.cloned.1.call-update) | async-done | bytes 2097168 | tf_op jit(solution)/shard_map/all_gather | solution.py:39
  58.3 38.5 %collective-permute-done.1 = f32[512,1024]{0,1:T(8,128)} collective-permute-done((f32[512,1024]{0,1:T(8,128)}, f32[512,1024]{0,1:T(8,128)}, u32[]{:S(2)}, u32[]{:S(2)}) %collective-permute-start.1) | collective-permute-done | bytes 2097184 | tf_op jit(solution)/shard_map/ppermute | solution.py:17
  102.2 5.6 pad_maximum_fusion
  107.8 6.5 copy.11
  114.3 5.6 gather_fusion
  119.9 5.5 fusion.17
  139.7 250.3 %all-reduce.8.cloned.1.call-done = (f32[512,512]{1,0:T(8,128)}, f32[2,512,32]{1,2,0:T(8,128)}) async-done(((f32[512,512]{1,0:T(8,128)}, f32[2,512,32]{1,2,0:T(8,128)}), (f32[512,512]{1,0:T(8,128)}, f32[2,512,32]{1,2,0:T(8,128)})) %all-reduce.8.cloned.1.call-update) | async-done | bytes 1179664 | tf_op jit(solution)/shard_map/psum | solution.py:90
  396.2 11.7 %cholesky.104 = f32[128,128]{1,0:T(8,128)S(1)} custom-call(f32[128,128]{1,0:T(8,128)S(1)} %cholesky.266), custom_call_target="Cholesky" | custom-call | tf_op jit(solution)/shard_map/jit(cholesky)/cholesky | solution.py:92
  407.9 9.8 custom-call.33
  422.1 11.7 %cholesky.217 = f32[128,128]{1,0:T(8,128)S(1)} custom-call(f32[128,128]{1,0:T(8,128)S(1)} %cholesky.270), custom_call_target="Cholesky" | custom-call | tf_op jit(solution)/shard_map/jit(cholesky)/cholesky | solution.py:92
  434.5 10.2 %custom-call.34 = f32[1,128,128]{1,2,0:T(8,128)S(1)} custom-call(f32[1,128,128]{2,1,0:T(8,128)S(1)} %get-tuple-element.61), custom_call_target="InvertDiagBlocksLowerTriangular" | custom-call | tf_op jit(solution)/shard_map/jit(cholesky)/cholesky | solution.py:92
  447.1 11.7 %cholesky.238 = f32[128,128]{1,0:T(8,128)S(1)} custom-call(f32[128,128]{1,0:T(8,128)S(1)} %cholesky.275), custom_call_target="Cholesky" | custom-call | tf_op jit(solution)/shard_map/jit(cholesky)/cholesky | solution.py:92
  460.2 9.8 custom-call.35
  472.3 11.7 %cholesky.255 = f32[128,128]{1,0:T(8,128)S(1)} custom-call(f32[128,128]{1,0:T(8,128)S(1)} %convolution_subtract_fusion.2), custom_call_target="Cholesky" | custom-call | tf_op jit(solution)/shard_map/jit(cholesky)/cholesky | solution.py:92
  491.1 12.0 %while.8 = (s32[]{:T(128)}, f32[512,512]{1,0:T(8,128)}, s32[4,2]{0,1:T(2,128)S(1)}, f32[4,128,128]{2,1,0:T(8,128)S(1)}, s32[]{:T(128)}) while((s32[]{:T(128)}, f32[512,512]{1,0:T(8,128)}, s32[4,2]{0,1:T(2,128)S(1)}, f32[4,128,128]{2,1,0:T(8,128)S(1)}, s32[]{:T(128)}) %tuple.51), condition=%wide.while_cond.1, body=%wide.while_body.1.sunk | while | flops 2 | bytes 131189 | solution.py:96
  503.1 39.3 %custom-call.39 = f32[4,128,128]{1,2,0:T(8,128)S(1)} custom-call(f32[4,128,128]{2,1,0:T(8,128)S(1)} %get-tuple-element.34), custom_call_target="InvertDiagBlocksLowerTriangular" | custom-call | tf_op jit(solution)/shard_map/triangular_solve/custom-call.8 | solution.py:96
  551.2 9.2 all_gather.14
  577.5 76.1 %all-reduce.1 = (f32[2,32]{1,0:T(2,128)S(1)}, f32[2,32]{1,0:T(2,128)S(1)}) all-reduce(f32[2,32]{1,0:T(2,128)S(1)} %dynamic_update_slice.22, f32[2,32]{1,0:T(2,128)S(1)} %dynamic_update_slice.21), channel_id=1, replica_groups=mesh['blk'=32,'leaf'=4,'samp'=2] {'blk','leaf','samp'}, use_global_device_ids=true, to_apply=%region_13.17 | all-reduce | flops 128 | bytes 1024 | tf_op jit(solution)/shard_map/psum | solution.py:79
  653.7 161.9 %all-reduce.6.cloned.1.call-done = f32[2,512,32]{1,2,0:T(8,128)} async-done(((f32[2,512,32]{1,2,0:T(8,128)}), f32[2,512,32]{1,2,0:T(8,128)}) %all-reduce.6.cloned.1.call-update) | async-done | bytes 131088 | tf_op jit(solution)/shard_map/psum | solution.py:79
  825.4 75.9 %psum.54 = f32[2,32]{1,0:T(2,128)S(1)} all-reduce(f32[2,32]{1,0:T(2,128)S(1)} %dynamic_update_slice.24), channel_id=1, replica_groups=mesh['blk'=32,'leaf'=4,'samp'=2] {'blk','leaf','samp'}, use_global_device_ids=true, to_apply=%region_16.20 | all-reduce | flops 64 | bytes 512 | tf_op jit(solution)/shard_map/psum | solution.py:79
  901.4 9.1 all_gather.15
  921.8 76.2 %psum.55 = f32[2,32]{1,0:T(2,128)S(1)} all-reduce(f32[2,32]{1,0:T(2,128)S(1)} %dynamic_update_slice.25), channel_id=1, replica_groups=mesh['blk'=32,'leaf'=4,'samp'=2] {'blk','leaf','samp'}, use_global_device_ids=true, to_apply=%region_18.22 | all-reduce | flops 64 | bytes 512 | tf_op jit(solution)/shard_map/psum | solution.py:79
  (152 shorter events, 114.0 us)
Async XLA Ops:
  7.2 39.9 %all-gather.2.cloned.1.call-start = ((), (), s32[]{:S(2)}) async-start(), calls=%async_computation | async-start | bytes 2621440 | tf_op jit(solution)/shard_map/all_gather | solution.py:39
  9.3 380.7 %all-reduce.8.cloned.1.call-start = ((), (), s32[]{:S(2)}) async-start(), calls=%async_computation.2 | async-start | bytes 2359296 | tf_op jit(solution)/shard_map/psum | solution.py:90
  19.9 33.9 %collective-permute-start.3 = (f32[3,1024]{1,0:T(4,128)S(1)}, f32[3,1024]{1,0:T(4,128)S(1)}, u32[]{:S(2)}, u32[]{:S(2)}) collective-permute-start(f32[3,1024]{1,0:T(4,128)S(1)} %all_gather.13), channel_id=1, source_target_pairs={{8,0},{16,8},{24,16},{32,24},{40,32},{48,40},{56,48},{64,56},{72,6... | collective-permute-start | bytes 36872 | tf_op jit(solution)/shard_map/ppermute | solution.py:17
  27.6 26.1 %collective-permute-start.2 = (f32[3,1024]{1,0:T(4,128)S(1)}, f32[3,1024]{1,0:T(4,128)S(1)}, u32[]{:S(2)}, u32[]{:S(2)}) collective-permute-start(f32[3,1024]{1,0:T(4,128)S(1)} %all_gather.13), channel_id=1, source_target_pairs={{248,0},{0,8},{8,16},{16,24},{24,32},{32,40},{40,48},{48,56},{56,6... | collective-permute-start | bytes 36872 | tf_op jit(solution)/shard_map/ppermute | solution.py:17
  47.1 49.8 %collective-permute-start.1 = (f32[512,1024]{0,1:T(8,128)}, f32[512,1024]{0,1:T(8,128)}, u32[]{:S(2)}, u32[]{:S(2)}) collective-permute-start(f32[512,1024]{0,1:T(8,128)} %all-gather.2.cloned.1.call-done), channel_id=1, source_target_pairs={{8,0},{16,8},{24,16},{32,24},{40,32},{48,40},{56,48},{64,56},{72,6... | collective-permute-start | bytes 6291464 | tf_op jit(solution)/shard_map/ppermute | solution.py:17
  52.2 50.0 %collective-permute-start = (f32[512,1024]{0,1:T(8,128)}, f32[512,1024]{0,1:T(8,128)}, u32[]{:S(2)}, u32[]{:S(2)}) collective-permute-start(f32[512,1024]{0,1:T(8,128)} %all-gather.2.cloned.1.call-done), channel_id=1, source_target_pairs={{248,0},{0,8},{8,16},{16,24},{24,32},{32,40},{40,48},{48,56},{56,6... | collective-permute-start | bytes 6291464 | tf_op jit(solution)/shard_map/ppermute | solution.py:17
  55.7 46.5 %copy-start.2 = (f32[512,1024]{0,1:T(8,128)S(1)}, f32[512,1024]{0,1:T(8,128)}, u32[]{:S(2)}) copy-start(f32[512,1024]{0,1:T(8,128)} %all-gather.2.cloned.1.call-done) | copy-start | bytes 6291460
  114.3 5.6 copy-start
  134.5 3.7 copy-start.5
  134.5 3.7 copy-start.10
  138.8 0.6 copy-start.7
  139.4 676.2 %all-reduce.6.cloned.1.call-start = ((), (), s32[]{:S(2)}) async-start(), calls=%async_computation.1 | async-start | bytes 262144 | tf_op jit(solution)/shard_map/psum | solution.py:79
  395.2 1.0 copy-start.1
  551.2 16.2 %copy-start.3 = (f32[32,256]{1,0:T(8,128)}, f32[32,256]{1,0:T(8,128)S(1)}, u32[]{:S(2)}) copy-start(f32[32,256]{1,0:T(8,128)S(1)} %convolution_subtract_fusion.4) | copy-start | bytes 98308
  560.4 7.0 collective-permute-start.5
  565.4 7.1 collective-permute-start.4
  573.2 80.4 %copy-start.6 = (f32[32,256]{1,0:T(8,128)S(1)}, f32[32,256]{1,0:T(8,128)}, u32[]{:S(2)}) copy-start(f32[32,256]{1,0:T(8,128)} %param.15) | copy-start | bytes 98308
  573.2 242.4 %copy-start.9 = (f32[2,512,32]{1,2,0:T(8,128)S(1)}, f32[2,512,32]{1,2,0:T(8,128)}, u32[]{:S(2)}) copy-start(f32[2,512,32]{1,2,0:T(8,128)} %get-tuple-element.50) | copy-start | bytes 393220
  576.1 325.3 %copy-start.4 = (f32[32,256]{1,0:T(8,128)S(1)}, f32[32,256]{1,0:T(8,128)}, u32[]{:S(2)}) copy-start(f32[32,256]{1,0:T(8,128)} %copy-done.3) | copy-start | bytes 98308
  576.7 0.7 copy-start.8
  910.5 4.0 collective-permute-start.7
  911.9 7.1 collective-permute-start.6
Sparse Core Ops, SparseCore 0:
  9.8 37.2 all-gather.1
  139.5 250.3 all-reduce.7
  577.5 238.0 all-reduce.5
where the time goes:
time: 1010 us
  waiting for transfers between devices  490 us (49%)
  blocking collectives  257 us (25%)
  other arithmetic  141 us (14%)
  matrix products  40.6 us (4%)
  local copies, waits for them, and re-layouts  40.1 us (4%)
  starting transfers between devices  20.1 us (2%)
  between operations  17.2 us (2%)
    psum x1, waiting for transfers between devices, local(): joint_gram, rhs_proj = lax.psum((joint_part, rhs_part), ALL_AXES)  250 us
    psum x3, blocking collectives, total_per_samp(): return jax.tree.map(unslot, lax.psum(jax.tree.map(slot, values), ALL_AXES))  228 us
    psum x1, waiting for transfers between devices, total_per_samp(): return jax.tree.map(unslot, lax.psum(jax.tree.map(slot, values), ALL_AXES))  162 us
    another operation x14, other arithmetic, local(): joint_factor = jnp.linalg.cholesky(joint_gram)  80.7 us
    ppermute x8, waiting for transfers between devices, shifted_2(): return lax.ppermute(block, axis, route)  57.9 us
    another operation x4, other arithmetic, precond_from(): lax.linalg.triangular_solve(joint_factor, first_solve, left_side=True, lo...  41.8 us
    all_gather x3, blocking collectives, beside_all(): slab_values = lax.all_gather(values, 'leaf', axis=1, tiled=True)  28.8 us
  transfers between devices with their start and end apart: 11, of which 9 were waited for; matrix products, arithmetic and copies ran while one was open for 1% of the time, Pallas kernels for 0%

commit v1 on v0

--- a/solution.py
+++ b/solution.py
@@ -36,7 +36,9 @@
 
 
 def beside_all(values):
-    slab_values = lax.all_gather(values, "leaf", axis=1, tiled=True)
+    lower = lax.psum(1, "leaf")
+    mixed_arr = jnp.concatenate(lower * [values], 1)
+    slab_values = lax.all_to_all(mixed_arr, "leaf", 1, 1, tiled=True)
     return jnp.concatenate([shifted(slab_values, 1), slab_values, shifted(slab_values, -1)], axis=1)
 
 

time: 1010 us -> 1010 us (level)
  waiting for transfers between devices: 490 us -> 465 us
  blocking collectives: 257 us -> 270 us
    all_to_all x0 -> x3, blocking collectives: none -> 45.5 us  [beside_all(): slab_values = lax.all_to_all(mixed_arr, 'leaf', 1, 1, tiled=True)]
    all_gather x3 -> x0, blocking collectives: 28.8 us -> none  [beside_all(): slab_values = lax.all_gather(values, 'leaf', axis=1, tiled=True)]
    all_gather x1 -> x0, waiting for transfers between devices: 19.4 us -> none  [beside_all(): slab_values = lax.all_gather(values, 'leaf', axis=1, tiled=True)]
where the time goes in v1:
time: 1010 us; the launch traced here: 1000 us
  waiting for transfers between devices  465 us (46%)
  blocking collectives  270 us (27%)
  other arithmetic  140 us (14%)
  local copies, waits for them, and re-layouts  42.7 us (4%)
  matrix products  40.6 us (4%)
  starting transfers between devices  24.7 us (2%)
  between operations  17.6 us (2%)
    psum x1, waiting for transfers between devices, local(): joint_gram, rhs_proj = lax.psum((joint_part, rhs_part), ALL_AXES)  250 us
    psum x3, blocking collectives, total_per_samp(): return jax.tree.map(unslot, lax.psum(jax.tree.map(slot, values), ALL_AXES))  224 us
    psum x1, waiting for transfers between devices, total_per_samp(): return jax.tree.map(unslot, lax.psum(jax.tree.map(slot, values), ALL_AXES))  161 us
    another operation x14, other arithmetic, local(): joint_factor = jnp.linalg.cholesky(joint_gram)  80.7 us
    ppermute x8, waiting for transfers between devices, shifted_2(): return lax.ppermute(block, axis, route)  49.6 us
    all_to_all x3, blocking collectives, beside_all(): slab_values = lax.all_to_all(mixed_arr, 'leaf', 1, 1, tiled=True)  45.5 us
    another operation x4, other arithmetic, precond_from(): lax.linalg.triangular_solve(joint_factor, first_solve, left_side=True, lo...  41.8 us
    ppermute x8, starting transfers between devices, shifted_2(): return lax.ppermute(block, axis, route)  21.1 us
  transfers between devices with their start and end apart: 11, of which 9 were waited for; matrix products, arithmetic and copies ran while one was open for 1% of the time, Pallas kernels for 0%

profile of v1, /device:TPU:1, one launch (start us, length us, event | category | flops | bytes accessed | tf_op | source)
XLA Modules:
  0.0 1000.5 jit_solution(16555393048090665377)
XLA Ops:
  10.6 29.6 %all_to_all.48 = f32[512,4,256]{2,0,1:T(8,128)S(1)} all-to-all(f32[512,4,256]{2,0,1:T(8,128)} %copy.20), channel_id=1, replica_groups=mesh['blk'=32,'leaf'=4,'samp'=2] {'leaf'}, dimensions={1} | all-to-all | bytes 4194304 | tf_op jit(solution)/shard_map/all_to_all | solution.py:41
  42.2 8.6 collective-permute-start.1
  64.2 30.2 %collective-permute-done.3 = f32[3,1024]{1,0:T(4,128)S(1)} collective-permute-done((f32[3,1024]{1,0:T(4,128)S(1)}, f32[3,1024]{1,0:T(4,128)S(1)}, u32[]{:S(2)}, u32[]{:S(2)}) %collective-permute-start.3) | collective-permute-done | bytes 12320 | tf_op jit(solution)/shard_map/ppermute | solution.py:17
  94.4 5.3 collective-permute-done.2
  109.5 5.9 pad_maximum_fusion
  115.4 5.7 gather_fusion
  121.1 5.5 fusion.17
  140.9 250.4 %all-reduce.8.cloned.1.call-done = (f32[512,512]{1,0:T(8,128)}, f32[2,512,32]{1,2,0:T(8,128)}) async-done(((f32[512,512]{1,0:T(8,128)}, f32[2,512,32]{1,2,0:T(8,128)}), (f32[512,512]{1,0:T(8,128)}, f32[2,512,32]{1,2,0:T(8,128)})) %all-reduce.8.cloned.1.call-update) | async-done | bytes 1179664 | tf_op jit(solution)/shard_map/psum | solution.py:92
  397.5 11.7 %cholesky.104 = f32[128,128]{1,0:T(8,128)S(1)} custom-call(f32[128,128]{1,0:T(8,128)S(1)} %cholesky.266), custom_call_target="Cholesky" | custom-call | tf_op jit(solution)/shard_map/jit(cholesky)/cholesky | solution.py:94
  409.3 9.8 custom-call.33
  423.5 11.7 %cholesky.217 = f32[128,128]{1,0:T(8,128)S(1)} custom-call(f32[128,128]{1,0:T(8,128)S(1)} %cholesky.270), custom_call_target="Cholesky" | custom-call | tf_op jit(solution)/shard_map/jit(cholesky)/cholesky | solution.py:94
  435.8 10.2 %custom-call.34 = f32[1,128,128]{1,2,0:T(8,128)S(1)} custom-call(f32[1,128,128]{2,1,0:T(8,128)S(1)} %get-tuple-element.61), custom_call_target="InvertDiagBlocksLowerTriangular" | custom-call | tf_op jit(solution)/shard_map/jit(cholesky)/cholesky | solution.py:94
  448.5 11.7 %cholesky.238 = f32[128,128]{1,0:T(8,128)S(1)} custom-call(f32[128,128]{1,0:T(8,128)S(1)} %cholesky.275), custom_call_target="Cholesky" | custom-call | tf_op jit(solution)/shard_map/jit(cholesky)/cholesky | solution.py:94
  461.5 9.8 custom-call.35
  473.6 11.7 %cholesky.255 = f32[128,128]{1,0:T(8,128)S(1)} custom-call(f32[128,128]{1,0:T(8,128)S(1)} %convolution_subtract_fusion.2), custom_call_target="Cholesky" | custom-call | tf_op jit(solution)/shard_map/jit(cholesky)/cholesky | solution.py:94
  492.4 12.0 %while.8 = (s32[]{:T(128)}, f32[512,512]{1,0:T(8,128)}, s32[4,2]{0,1:T(2,128)S(1)}, f32[4,128,128]{2,1,0:T(8,128)S(1)}, s32[]{:T(128)}) while((s32[]{:T(128)}, f32[512,512]{1,0:T(8,128)}, s32[4,2]{0,1:T(2,128)S(1)}, f32[4,128,128]{2,1,0:T(8,128)S(1)}, s32[]{:T(128)}) %tuple.51), condition=%wide.while_cond.1, body=%wide.while_body.1.sunk | while | flops 2 | bytes 131189 | solution.py:98
  504.4 39.3 %custom-call.39 = f32[4,128,128]{1,2,0:T(8,128)S(1)} custom-call(f32[4,128,128]{2,1,0:T(8,128)S(1)} %get-tuple-element.34), custom_call_target="InvertDiagBlocksLowerTriangular" | custom-call | tf_op jit(solution)/shard_map/triangular_solve/custom-call.8 | solution.py:98
  552.5 8.7 all_to_all.49
  561.2 5.4 collective-permute-start.5
  578.6 73.9 %all-reduce.1 = (f32[2,32]{1,0:T(2,128)S(1)}, f32[2,32]{1,0:T(2,128)S(1)}) all-reduce(f32[2,32]{1,0:T(2,128)S(1)} %dynamic_update_slice.22, f32[2,32]{1,0:T(2,128)S(1)} %dynamic_update_slice.21), channel_id=1, replica_groups=mesh['blk'=32,'leaf'=4,'samp'=2] {'blk','leaf','samp'}, use_global_device_ids=true, to_apply=%region_13.17 | all-reduce | flops 128 | bytes 1024 | tf_op jit(solution)/shard_map/psum | solution.py:81
  652.6 161.3 %all-reduce.6.cloned.1.call-done = f32[2,512,32]{1,2,0:T(8,128)} async-done(((f32[2,512,32]{1,2,0:T(8,128)}), f32[2,512,32]{1,2,0:T(8,128)}) %all-reduce.6.cloned.1.call-update) | async-done | bytes 131088 | tf_op jit(solution)/shard_map/psum | solution.py:81
  823.7 75.9 %psum.54 = f32[2,32]{1,0:T(2,128)S(1)} all-reduce(f32[2,32]{1,0:T(2,128)S(1)} %dynamic_update_slice.24), channel_id=1, replica_groups=mesh['blk'=32,'leaf'=4,'samp'=2] {'blk','leaf','samp'}, use_global_device_ids=true, to_apply=%region_16.20 | all-reduce | flops 64 | bytes 512 | tf_op jit(solution)/shard_map/psum | solution.py:81
  899.7 7.2 all_to_all.50
  918.3 74.4 %psum.55 = f32[2,32]{1,0:T(2,128)S(1)} all-reduce(f32[2,32]{1,0:T(2,128)S(1)} %dynamic_update_slice.25), channel_id=1, replica_groups=mesh['blk'=32,'leaf'=4,'samp'=2] {'blk','leaf','samp'}, use_global_device_ids=true, to_apply=%region_18.22 | all-reduce | flops 64 | bytes 512 | tf_op jit(solution)/shard_map/psum | solution.py:81
  (168 shorter events, 118.9 us)
Async XLA Ops:
  40.1 2.1 copy-start
  40.1 10.7 %copy-start.11 = (f32[3,256]{1,0:T(4,128)S(1)}, f32[3,256]{1,0:T(4,128)}, u32[]{:S(2)}) copy-start(f32[3,256]{1,0:T(4,128)} %param.11) | copy-start | bytes 9220
  40.1 14.6 %copy-start.12 = (s32[1,8]{1,0:T(1,128)S(1)}, s32[1,8]{1,0:T(1,128)}, u32[]{:S(2)}) copy-start(s32[1,8]{1,0:T(1,128)} %param.12) | copy-start | bytes 100
  42.2 61.4 %collective-permute-start.1 = (f32[512,1024]{0,1:T(8,128)}, f32[512,1024]{0,1:T(8,128)}, u32[]{:S(2)}, u32[]{:S(2)}) collective-permute-start(f32[512,1024]{0,1:T(8,128)} %bitcast.233), channel_id=1, source_target_pairs={{8,0},{16,8},{24,16},{32,24},{40,32},{48,40},{56,48},{64,56},{72,6... | collective-permute-start | bytes 6291464 | tf_op jit(solution)/shard_map/ppermute | solution.py:17
  50.8 55.8 %collective-permute-start = (f32[512,1024]{0,1:T(8,128)}, f32[512,1024]{0,1:T(8,128)}, u32[]{:S(2)}, u32[]{:S(2)}) collective-permute-start(f32[512,1024]{0,1:T(8,128)} %bitcast.234), channel_id=1, source_target_pairs={{248,0},{0,8},{8,16},{16,24},{24,32},{32,40},{40,48},{48,56},{56,6... | collective-permute-start | bytes 6291464 | tf_op jit(solution)/shard_map/ppermute | solution.py:17
  51.4 7.4 all-to-all-start.1
  54.7 336.6 %all-reduce.8.cloned.1.call-start = ((), (), s32[]{:S(2)}) async-start(), calls=%async_computation.5 | async-start | bytes 2359296 | tf_op jit(solution)/shard_map/psum | solution.py:92
  58.9 35.6 %collective-permute-start.3 = (f32[3,1024]{1,0:T(4,128)S(1)}, f32[3,1024]{1,0:T(4,128)S(1)}, u32[]{:S(2)}, u32[]{:S(2)}) collective-permute-start(f32[3,1024]{1,0:T(4,128)S(1)} %bitcast.253), channel_id=1, source_target_pairs={{8,0},{16,8},{24,16},{32,24},{40,32},{48,40},{56,48},{64,56},{72,6... | collective-permute-start | bytes 36872 | tf_op jit(solution)/shard_map/ppermute | solution.py:17
  64.1 35.7 %collective-permute-start.2 = (f32[3,1024]{1,0:T(4,128)S(1)}, f32[3,1024]{1,0:T(4,128)S(1)}, u32[]{:S(2)}, u32[]{:S(2)}) collective-permute-start(f32[3,1024]{1,0:T(4,128)S(1)} %bitcast.254), channel_id=1, source_target_pairs={{248,0},{0,8},{8,16},{16,24},{24,32},{32,40},{40,48},{48,56},{56,6... | collective-permute-start | bytes 36872 | tf_op jit(solution)/shard_map/ppermute | solution.py:17
  115.4 5.7 copy-start.1
  135.7 3.7 copy-start.5
  135.7 3.7 copy-start.10
  140.0 0.6 copy-start.7
  140.6 673.2 %all-reduce.6.cloned.1.call-start = ((), (), s32[]{:S(2)}) async-start(), calls=%async_computation.4 | async-start | bytes 262144 | tf_op jit(solution)/shard_map/psum | solution.py:81
  396.5 1.0 copy-start.2
  552.5 21.3 %copy-start.3 = (f32[32,256]{1,0:T(8,128)}, f32[32,256]{1,0:T(8,128)S(1)}, u32[]{:S(2)}) copy-start(f32[32,256]{1,0:T(8,128)S(1)} %convolution_subtract_fusion.4) | copy-start | bytes 98308
  561.2 7.3 collective-permute-start.5
  566.6 7.1 collective-permute-start.4
  574.4 78.2 %copy-start.6 = (f32[32,256]{1,0:T(8,128)S(1)}, f32[32,256]{1,0:T(8,128)}, u32[]{:S(2)}) copy-start(f32[32,256]{1,0:T(8,128)} %param.15) | copy-start | bytes 98308
  574.4 239.5 %copy-start.9 = (f32[2,512,32]{1,2,0:T(8,128)S(1)}, f32[2,512,32]{1,2,0:T(8,128)}, u32[]{:S(2)}) copy-start(f32[2,512,32]{1,2,0:T(8,128)} %get-tuple-element.50) | copy-start | bytes 393220
  577.2 322.4 %copy-start.4 = (f32[32,256]{1,0:T(8,128)S(1)}, f32[32,256]{1,0:T(8,128)}, u32[]{:S(2)}) copy-start(f32[32,256]{1,0:T(8,128)} %copy-done.3) | copy-start | bytes 98308
  577.8 0.7 copy-start.8
  907.0 4.1 collective-permute-start.7
  908.5 7.1 collective-permute-start.6
Sparse Core Ops, SparseCore 0:
  140.8 250.4 all-reduce.7
  578.6 235.1 all-reduce.5
